TPU v7x, 32 devices: a whole 2x2x4 slice. The times are simulated.
32 devices in a mesh: row: 8 (over z, x), col: 4 (over y, core).
Axes of the slice: x: 2, y: 2, z: 4, core: 2. Of those that a mesh axis runs over, the one named last changes fastest.
Arguments:
- matrix: float32 [8192, 4096], P('row', 'col'), may hold values from -6 to 6
- tile_mask: int32 [64, 32], P('row', 'col'), may hold values 0 or 1
- panel_order: int32 [32], replicated, may hold values from 0 to 31, each once
Outputs:
- factors: float32 [4, 128, 128], replicated
- projections: float32 [4, 128, 4096], P(None, None, 'col')
- remainder: float32 [8192, 4096], P('row', 'col')
Inputs may be any that keep to these rules, and one draw needn't show every extreme that they name: panel_order is a permutation of the column blocks, so the 4 panels differ, and every column block among the first 4 of panel_order has at least one nonzero tile in tile_mask.
All inputs are finite; a program needn't handle non-finite values. No bound on the sum of `tile_mask` on one device may be relied on, other than what follows from the above.
Results may differ from a plain program's by a relative error of at most 0.0001.
Values sent between devices are 32-bit elements; how exact they have to be, the bound alone decides.
No kernel may reach another device: no remote copies, remote signals or barrier semaphores. Data moves between devices by JAX's collectives and lax.ppermute only.
A program may use at most 64 MiB of HBM per device.

v0:
```python
import jax
import jax.numpy as jnp
from jax import lax
from jax.sharding import PartitionSpec as P

PANELS = 4


def from_root(array, axis, root):
    mine = lax.axis_index(axis) == root
    return lax.psum(jnp.where(mine, array, jnp.zeros_like(array)), axis)


def apply_basis(basis_t, proj):
    return lax.dot_general(basis_t, proj, (((0,), (0,)), ((), ())), precision=lax.Precision.HIGHEST)


def fetch(block, owner):
    return from_root(block, "col", owner)


def on_device(matrix, tile_mask, panel_order):
    hi = lax.Precision.HIGHEST
    rows, cols = matrix.shape
    nb_local = tile_mask.shape[1]
    tile = cols // nb_local
    work = (
        matrix.reshape(rows // tile, tile, nb_local, tile)
        * tile_mask.astype(jnp.float32)[:, None, :, None]
    ).reshape(rows, cols)
    first = panel_order[0]
    panel = fetch(
        lax.dynamic_slice_in_dim(work, first % nb_local * tile, tile, 1), first // nb_local
    )
    factor_list = []
    proj_list = []
    for p in range(PANELS):
        gram = lax.psum(jnp.dot(panel.T, panel, precision=hi), "row")
        lower = jnp.linalg.cholesky(gram)
        basis_t = jax.scipy.linalg.solve_triangular(lower, panel.T, lower=True)
        proj = lax.psum(jnp.dot(basis_t, work, precision=hi), "row")
        factor_list.append(lower.T)
        proj_list.append(proj)
        if p + 1 < PANELS:
            following = panel_order[p + 1]
            start = following % nb_local * tile
            work = work - apply_basis(basis_t, proj)
            panel = fetch(lax.dynamic_slice_in_dim(work, start, tile, 1), following // nb_local)
        else:
            work = work - apply_basis(basis_t, proj)
    return (jnp.stack(factor_list), jnp.stack(proj_list), work)


def solution(mesh):
    return jax.shard_map(
        on_device,
        mesh=mesh,
        in_specs=(P("row", "col"), P("row", "col"), P()),
        out_specs=(P(), P(None, None, "col"), P("row", "col")),
        check_vma=False,
    )
```

profile of v0, /device:TPU:0, one launch (start us, length us, event | category | flops | bytes accessed | tf_op | source)
XLA Modules:
  0.0 906.0 jit_solution(16287603222332352959)
XLA Ops:
  7.2 1.5 fusion.20
  11.3 0.7 convert_element_type.3
  12.3 1.8 copy-done.5
  14.2 1.5 bitcast_multiply_fusion
  15.7 2.0 copy-done.2
  17.7 0.9 dynamic-slice_select_fusion.3
  18.6 36.3 %all-reduce.13.cloned.1.call-done = f32[1024,128]{1,0:T(8,128)} async-done(((f32[1024,128]{1,0:T(8,128)}), f32[1024,128]{1,0:T(8,128)}) %all-reduce.13.cloned.1.call-update) | async-done | bytes 524304 | tf_op jit(solution)/shard_map/psum | solution.py:11
  54.9 2.8 fusion.21
  58.0 70.3 %all-reduce.15.cloned.1.call-done = f32[128,128]{0,1:T(8,128)} async-done(((f32[128,128]{0,1:T(8,128)}), f32[128,128]{0,1:T(8,128)}) %all-reduce.15.cloned.1.call-update) | async-done | bytes 65552 | tf_op jit(solution)/shard_map/psum | solution.py:38
  128.3 0.9 copy.7
  129.2 0.9 fusion.15
  130.1 11.7 %cholesky.74 = f32[128,128]{1,0:T(8,128)S(1)} custom-call(f32[128,128]{1,0:T(8,128)S(1)} %fusion.15), custom_call_target="Cholesky" | custom-call | tf_op jit(solution)/shard_map/jit(cholesky)/cholesky | solution.py:39
  141.8 0.6 compare_reduce_fusion.3
  142.5 0.7 fusion.16
  143.1 9.8 %custom-call.8 = f32[1,128,128]{1,2,0:T(8,128)S(1)} custom-call(f32[1,128,128]{2,1,0:T(8,128)S(1)} %get-tuple-element.11), custom_call_target="InvertDiagBlocksLowerTriangular" | custom-call | tf_op jit(solution)/shard_map/jit(_solve_triangular)/triangular_solve | solution.py:40
  153.0 1.7 fusion.6
  154.6 5.4 fusion.22
  162.9 70.0 %all-reduce.17.cloned.1.call-done = f32[128,1024]{1,0:T(8,128)} async-done(((f32[128,1024]{1,0:T(8,128)}), f32[128,1024]{1,0:T(8,128)}) %all-reduce.17.cloned.1.call-update) | async-done | bytes 524304 | tf_op jit(solution)/shard_map/psum | solution.py:41
  232.9 5.5 convolution_subtract_fusion.3
  238.4 2.0 copy-done.1
  240.4 0.9 dynamic-slice_select_fusion.2
  241.3 32.7 %all-reduce.19.cloned.1.call-done = f32[1024,128]{1,0:T(8,128)} async-done(((f32[1024,128]{1,0:T(8,128)}), f32[1024,128]{1,0:T(8,128)}) %all-reduce.19.cloned.1.call-update) | async-done | bytes 524304 | tf_op jit(solution)/shard_map/psum | solution.py:11
  274.0 2.8 fusion.23
  277.2 70.1 %all-reduce.21.cloned.1.call-done = f32[128,128]{0,1:T(8,128)} async-done(((f32[128,128]{0,1:T(8,128)}), f32[128,128]{0,1:T(8,128)}) %all-reduce.21.cloned.1.call-update) | async-done | bytes 65552 | tf_op jit(solution)/shard_map/psum | solution.py:38
  347.3 0.9 copy.9
  348.2 0.9 fusion.13
  349.1 11.7 %cholesky.85 = f32[128,128]{1,0:T(8,128)S(1)} custom-call(f32[128,128]{1,0:T(8,128)S(1)} %fusion.13), custom_call_target="Cholesky" | custom-call | tf_op jit(solution)/shard_map/jit(cholesky)/cholesky | solution.py:39
  360.8 0.6 compare_reduce_fusion.2
  361.5 0.7 fusion.17
  362.1 9.8 %custom-call.9 = f32[1,128,128]{1,2,0:T(8,128)S(1)} custom-call(f32[1,128,128]{2,1,0:T(8,128)S(1)} %get-tuple-element.13), custom_call_target="InvertDiagBlocksLowerTriangular" | custom-call | tf_op jit(solution)/shard_map/jit(_solve_triangular)/triangular_solve | solution.py:40
  371.9 1.7 fusion.4
  373.6 5.4 fusion.24
  381.4 70.4 %all-reduce.23.cloned.1.call-done = f32[128,1024]{1,0:T(8,128)} async-done(((f32[128,1024]{1,0:T(8,128)}), f32[128,1024]{1,0:T(8,128)}) %all-reduce.23.cloned.1.call-update) | async-done | bytes 524304 | tf_op jit(solution)/shard_map/psum | solution.py:41
  451.8 5.5 convolution_subtract_fusion.2
  457.3 2.0 copy-done
  459.3 0.9 dynamic-slice_select_fusion.1
  460.2 32.7 %all-reduce.25.cloned.1.call-done = f32[1024,128]{1,0:T(8,128)} async-done(((f32[1024,128]{1,0:T(8,128)}), f32[1024,128]{1,0:T(8,128)}) %all-reduce.25.cloned.1.call-update) | async-done | bytes 524304 | tf_op jit(solution)/shard_map/psum | solution.py:11
  492.9 2.8 fusion.25
  496.2 70.1 %all-reduce.27.cloned.1.call-done = f32[128,128]{0,1:T(8,128)} async-done(((f32[128,128]{0,1:T(8,128)}), f32[128,128]{0,1:T(8,128)}) %all-reduce.27.cloned.1.call-update) | async-done | bytes 65552 | tf_op jit(solution)/shard_map/psum | solution.py:38
  566.3 0.9 copy.11
  567.2 0.9 fusion.11
  568.1 11.7 %cholesky.96 = f32[128,128]{1,0:T(8,128)S(1)} custom-call(f32[128,128]{1,0:T(8,128)S(1)} %fusion.11), custom_call_target="Cholesky" | custom-call | tf_op jit(solution)/shard_map/jit(cholesky)/cholesky | solution.py:39
  580.5 0.7 fusion.18
  581.2 9.8 %custom-call.10 = f32[1,128,128]{1,2,0:T(8,128)S(1)} custom-call(f32[1,128,128]{2,1,0:T(8,128)S(1)} %get-tuple-element.15), custom_call_target="InvertDiagBlocksLowerTriangular" | custom-call | tf_op jit(solution)/shard_map/jit(_solve_triangular)/triangular_solve | solution.py:40
  591.0 1.7 fusion.2
  592.7 5.4 fusion.26
  600.3 70.6 %all-reduce.29.cloned.1.call-done = f32[128,1024]{1,0:T(8,128)} async-done(((f32[128,1024]{1,0:T(8,128)}), f32[128,1024]{1,0:T(8,128)}) %all-reduce.29.cloned.1.call-update) | async-done | bytes 524304 | tf_op jit(solution)/shard_map/psum | solution.py:41
  671.0 5.5 convolution_subtract_fusion.1
  676.5 2.0 copy-done.3
  678.5 0.9 dynamic-slice_select_fusion
  679.4 32.7 %all-reduce.31.cloned.1.call-done = f32[1024,128]{1,0:T(8,128)} async-done(((f32[1024,128]{1,0:T(8,128)}), f32[1024,128]{1,0:T(8,128)}) %all-reduce.31.cloned.1.call-update) | async-done | bytes 524304 | tf_op jit(solution)/shard_map/psum | solution.py:11
  712.1 2.9 fusion.27
  715.2 70.3 %all-reduce.33.cloned.1.call-done = f32[128,128]{0,1:T(8,128)} async-done(((f32[128,128]{0,1:T(8,128)}), f32[128,128]{0,1:T(8,128)}) %all-reduce.33.cloned.1.call-update) | async-done | bytes 65552 | tf_op jit(solution)/shard_map/psum | solution.py:38
  785.5 0.9 copy.13
  786.4 1.0 fusion.9
  787.4 11.7 %cholesky.107 = f32[128,128]{1,0:T(8,128)S(1)} custom-call(f32[128,128]{1,0:T(8,128)S(1)} %fusion.9), custom_call_target="Cholesky" | custom-call | tf_op jit(solution)/shard_map/jit(cholesky)/cholesky | solution.py:39
  799.8 0.7 select_bitcast_fusion
  800.5 9.8 %custom-call.11 = f32[1,128,128]{1,2,0:T(8,128)S(1)} custom-call(f32[1,128,128]{2,1,0:T(8,128)S(1)} %get-tuple-element.8), custom_call_target="InvertDiagBlocksLowerTriangular" | custom-call | tf_op jit(solution)/shard_map/jit(_solve_triangular)/triangular_solve | solution.py:40
  810.3 1.7 fusion
  812.0 5.4 fusion.28
  817.4 0.8 copy.14
  818.3 71.9 %all-reduce.35.cloned.1.call-done = f32[128,1024]{1,0:T(8,128)} async-done(((f32[128,1024]{1,0:T(8,128)}), f32[128,1024]{1,0:T(8,128)}) %all-reduce.35.cloned.1.call-update) | async-done | bytes 524304 | tf_op jit(solution)/shard_map/psum | solution.py:41
  890.2 2.7 pad_maximum_fusion
  892.8 6.1 convolution_subtract_fusion
  (45 shorter events, 3.5 us)
Async XLA Ops:
  7.2 47.7 %all-reduce.13.cloned.1.call-start = ((), (), s32[]{:S(2)}) async-start(), calls=%async_computation | async-start | bytes 1048576 | tf_op jit(solution)/shard_map/psum | solution.py:11
  12.0 2.2 copy-start.5
  15.7 2.0 copy-start.2
  18.6 109.7 %all-reduce.15.cloned.1.call-start = ((), (), s32[]{:S(2)}) async-start(), calls=%async_computation.1 | async-start | bytes 131072 | tf_op jit(solution)/shard_map/psum | solution.py:38
  57.8 175.1 %all-reduce.17.cloned.1.call-start = ((), (), s32[]{:S(2)}) async-start(), calls=%async_computation.2 | async-start | bytes 1048576 | tf_op jit(solution)/shard_map/psum | solution.py:41
  160.1 114.0 %all-reduce.19.cloned.1.call-start = ((), (), s32[]{:S(2)}) async-start(), calls=%async_computation.3 | async-start | bytes 1048576 | tf_op jit(solution)/shard_map/psum | solution.py:11
  238.4 2.0 copy-start.1
  241.3 106.0 %all-reduce.21.cloned.1.call-start = ((), (), s32[]{:S(2)}) async-start(), calls=%async_computation.4 | async-start | bytes 131072 | tf_op jit(solution)/shard_map/psum | solution.py:38
  276.9 174.9 %all-reduce.23.cloned.1.call-start = ((), (), s32[]{:S(2)}) async-start(), calls=%async_computation.5 | async-start | bytes 1048576 | tf_op jit(solution)/shard_map/psum | solution.py:41
  379.0 113.9 %all-reduce.25.cloned.1.call-start = ((), (), s32[]{:S(2)}) async-start(), calls=%async_computation.6 | async-start | bytes 1048576 | tf_op jit(solution)/shard_map/psum | solution.py:11
  457.3 2.0 copy-start
  460.2 106.1 %all-reduce.27.cloned.1.call-start = ((), (), s32[]{:S(2)}) async-start(), calls=%async_computation.7 | async-start | bytes 131072 | tf_op jit(solution)/shard_map/psum | solution.py:38
  495.8 175.2 %all-reduce.29.cloned.1.call-start = ((), (), s32[]{:S(2)}) async-start(), calls=%async_computation.8 | async-start | bytes 1048576 | tf_op jit(solution)/shard_map/psum | solution.py:41
  598.1 114.0 %all-reduce.31.cloned.1.call-start = ((), (), s32[]{:S(2)}) async-start(), calls=%async_computation.9 | async-start | bytes 1048576 | tf_op jit(solution)/shard_map/psum | solution.py:11
  676.5 2.0 copy-start.3
  679.4 106.1 %all-reduce.33.cloned.1.call-start = ((), (), s32[]{:S(2)}) async-start(), calls=%async_computation.10 | async-start | bytes 131072 | tf_op jit(solution)/shard_map/psum | solution.py:38
  715.0 175.2 %all-reduce.35.cloned.1.call-start = ((), (), s32[]{:S(2)}) async-start(), calls=%async_computation.11 | async-start | bytes 1048576 | tf_op jit(solution)/shard_map/psum | solution.py:41
  786.4 103.7 %copy-start.6 = (f32[128,1024]{1,0:T(8,128)S(1)}, f32[128,1024]{1,0:T(8,128)}, u32[]{:S(2)}) copy-start(f32[128,1024]{1,0:T(8,128)} %all-reduce.17.cloned.1.call-done) | copy-start | bytes 1572868
  786.4 103.7 %copy-start.7 = (f32[128,1024]{1,0:T(8,128)S(1)}, f32[128,1024]{1,0:T(8,128)}, u32[]{:S(2)}) copy-start(f32[128,1024]{1,0:T(8,128)} %all-reduce.23.cloned.1.call-done) | copy-start | bytes 1572868
  786.4 103.7 %copy-start.8 = (f32[128,1024]{1,0:T(8,128)S(1)}, f32[128,1024]{1,0:T(8,128)}, u32[]{:S(2)}) copy-start(f32[128,1024]{1,0:T(8,128)} %all-reduce.29.cloned.1.call-done) | copy-start | bytes 1572868
  890.2 2.7 copy-start.4
Sparse Core Ops, SparseCore 0:
  18.7 36.1 all-reduce.12
  58.9 69.3 all-reduce.14
  160.2 72.6 all-reduce.16
  241.4 32.5 all-reduce.18
  277.9 69.3 all-reduce.20
  379.2 72.6 all-reduce.22
  460.3 32.5 all-reduce.24
  496.9 69.3 all-reduce.26
  598.2 72.7 all-reduce.28
  679.5 32.5 all-reduce.30
  716.1 69.3 all-reduce.32
  817.5 72.6 all-reduce.34
where the time goes:
time: 910 us; the launch traced here: 906 us
  waiting for transfers between devices  698 us (77%)
  other arithmetic  103 us (11%)
  matrix products  62.2 us (7%)
  between operations  24.5 us (3%)
  local copies, waits for them, and re-layouts  16.2 us (2%)
    psum x4, waiting for transfers between devices, on_device(): proj = lax.psum(jnp.dot(basis_t, work, precision=hi), 'row')  283 us
    psum x4, waiting for transfers between devices, on_device(): gram = lax.psum(jnp.dot(panel.T, panel, precision=hi), 'row')  281 us
    psum x4, waiting for transfers between devices, from_root(): return lax.psum(jnp.where(mine, array, jnp.zeros_like(array)), axis)  134 us
    another operation x12, other arithmetic, on_device(): lower = jnp.linalg.cholesky(gram)  49.6 us
    another operation x5, other arithmetic, on_device(): basis_t = jax.scipy.linalg.solve_triangular(lower, panel.T, lower=True)  39.9 us
    dot_general x4, matrix products, apply_basis(): lax.dot_general(basis_t, proj, (((0,), (0,)), ((), ())), precision=lax.Pr...  22.5 us
    dot_general x4, matrix products, on_device(): proj = lax.psum(jnp.dot(basis_t, work, precision=hi), 'row')  21.5 us
  transfers between devices with their start and end apart: 12, of which 12 were waited for; matrix products, arithmetic and copies ran while one was open for 0% of the time, Pallas kernels for 0%

commit v1 on v0

--- a/solution.py
+++ b/solution.py
@@ -8,7 +8,7 @@
 
 def from_root(array, axis, root):
     mine = lax.axis_index(axis) == root
-    return lax.psum(jnp.where(mine, array, jnp.zeros_like(array)), axis)
+    return jnp.sum(lax.all_gather(jnp.where(mine, array, jnp.zeros_like(array)), axis), axis=0)
 
 
 def apply_basis(basis_t, proj):

time: 910 us -> 862 us (0.947)
  waiting for transfers between devices: 698 us -> 653 us
  matrix products: 62.2 us -> 53.1 us
    psum x4 -> x0, waiting for transfers between devices: 134 us -> none  [from_root(): return lax.psum(jnp.where(mine, array, jnp.zeros_like(array)), axis)]
    all_gather x0 -> x4, waiting for transfers between devices: none -> 90.6 us  [from_root(): lax.all_gather(jnp.where(mine, array, jnp.zeros_like(array)), axis)]
where the time goes in v1:
time: 862 us; the launch traced here: 858 us
  waiting for transfers between devices  653 us (76%)
  other arithmetic  110 us (13%)
  matrix products  53.1 us (6%)
  between operations  24.3 us (3%)
  local copies, waits for them, and re-layouts  16.2 us (2%)
    psum x4, waiting for transfers between devices, on_device(): proj = lax.psum(jnp.dot(basis_t, work, precision=hi), 'row')  283 us
    psum x4, waiting for transfers between devices, on_device(): gram = lax.psum(jnp.dot(panel.T, panel, precision=hi), 'row')  279 us
    all_gather x4, waiting for transfers between devices, from_root(): lax.all_gather(jnp.where(mine, array, jnp.zeros_like(array)), axis)  90.6 us
    another operation x12, other arithmetic, on_device(): lower = jnp.linalg.cholesky(gram)  49.6 us
    another operation x5, other arithmetic, on_device(): basis_t = jax.scipy.linalg.solve_triangular(lower, panel.T, lower=True)  39.9 us
    dot_general x4, matrix products, apply_basis(): lax.dot_general(basis_t, proj, (((0,), (0,)), ((), ())), precision=lax.Pr...  22.5 us
    dot_general x4, matrix products, on_device(): proj = lax.psum(jnp.dot(basis_t, work, precision=hi), 'row')  21.5 us
  transfers between devices with their start and end apart: 12, of which 12 were waited for; matrix products, arithmetic and copies ran while one was open for 0% of the time, Pallas kernels for 0%

profile of v1, /device:TPU:0, one launch (start us, length us, event | category | flops | bytes accessed | tf_op | source)
XLA Modules:
  0.0 858.0 jit_solution(9509730356401213892)
XLA Ops:
  7.2 1.4 fusion.20
  11.2 0.7 convert_element_type.3
  12.3 1.8 copy-done.5
  14.1 1.5 bitcast_multiply_fusion
  15.6 2.0 copy-done.2
  17.7 0.9 dynamic-slice_select_fusion.3
  18.6 25.4 %all-gather.9.cloned.1.call-done = f32[4096,128]{1,0:T(8,128)} async-done(((f32[1024,128]{1,0:T(8,128)}), f32[4096,128]{1,0:T(8,128)}) %all-gather.9.cloned.1.call-update) | async-done | bytes 2097168 | tf_op jit(solution)/shard_map/all_gather | solution.py:11
  44.0 1.8 reduce_sum.36
  45.7 1.6 fusion.21
  47.6 69.6 %all-reduce.9.cloned.1.call-done = f32[128,128]{0,1:T(8,128)} async-done(((f32[128,128]{0,1:T(8,128)}), f32[128,128]{0,1:T(8,128)}) %all-reduce.9.cloned.1.call-update) | async-done | bytes 65552 | tf_op jit(solution)/shard_map/psum | solution.py:38
  117.3 0.9 copy.7
  118.2 0.9 fusion.15
  119.1 11.7 %cholesky.74 = f32[128,128]{1,0:T(8,128)S(1)} custom-call(f32[128,128]{1,0:T(8,128)S(1)} %fusion.15), custom_call_target="Cholesky" | custom-call | tf_op jit(solution)/shard_map/jit(cholesky)/cholesky | solution.py:39
  130.8 0.6 compare_reduce_fusion.3
  131.5 0.7 fusion.16
  132.1 9.8 %custom-call.8 = f32[1,128,128]{1,2,0:T(8,128)S(1)} custom-call(f32[1,128,128]{2,1,0:T(8,128)S(1)} %get-tuple-element.11), custom_call_target="InvertDiagBlocksLowerTriangular" | custom-call | tf_op jit(solution)/shard_map/jit(_solve_triangular)/triangular_solve | solution.py:40
  142.6 5.4 fusion.22
  150.6 70.4 %all-reduce.11.cloned.1.call-done = f32[128,1024]{1,0:T(8,128)} async-done(((f32[128,1024]{1,0:T(8,128)}), f32[128,1024]{1,0:T(8,128)}) %all-reduce.11.cloned.1.call-update) | async-done | bytes 524304 | tf_op jit(solution)/shard_map/psum | solution.py:41
  220.9 5.5 convolution_subtract_fusion.3
  226.4 2.0 copy-done.1
  228.4 0.9 dynamic-slice_select_fusion.2
  229.7 21.5 %all-gather.11.cloned.1.call-done = f32[4096,128]{1,0:T(8,128)} async-done(((f32[1024,128]{1,0:T(8,128)}), f32[4096,128]{1,0:T(8,128)}) %all-gather.11.cloned.1.call-update) | async-done | bytes 2097168 | tf_op jit(solution)/shard_map/all_gather | solution.py:11
  251.2 1.8 reduce_sum.37
  253.0 1.6 fusion.23
  254.7 69.6 %all-reduce.13.cloned.1.call-done = f32[128,128]{0,1:T(8,128)} async-done(((f32[128,128]{0,1:T(8,128)}), f32[128,128]{0,1:T(8,128)}) %all-reduce.13.cloned.1.call-update) | async-done | bytes 65552 | tf_op jit(solution)/shard_map/psum | solution.py:38
  324.3 0.9 copy.9
  325.2 0.9 fusion.13
  326.1 11.7 %cholesky.85 = f32[128,128]{1,0:T(8,128)S(1)} custom-call(f32[128,128]{1,0:T(8,128)S(1)} %fusion.13), custom_call_target="Cholesky" | custom-call | tf_op jit(solution)/shard_map/jit(cholesky)/cholesky | solution.py:39
  337.8 0.6 compare_reduce_fusion.2
  338.5 0.7 fusion.17
  339.2 9.8 %custom-call.9 = f32[1,128,128]{1,2,0:T(8,128)S(1)} custom-call(f32[1,128,128]{2,1,0:T(8,128)S(1)} %get-tuple-element.13), custom_call_target="InvertDiagBlocksLowerTriangular" | custom-call | tf_op jit(solution)/shard_map/jit(_solve_triangular)/triangular_solve | solution.py:40
  349.6 5.4 fusion.24
  357.3 70.5 %all-reduce.15.cloned.1.call-done = f32[128,1024]{1,0:T(8,128)} async-done(((f32[128,1024]{1,0:T(8,128)}), f32[128,1024]{1,0:T(8,128)}) %all-reduce.15.cloned.1.call-update) | async-done | bytes 524304 | tf_op jit(solution)/shard_map/psum | solution.py:41
  427.8 5.5 convolution_subtract_fusion.2
  433.3 2.0 copy-done
  435.3 0.9 dynamic-slice_select_fusion.1
  436.2 21.9 %all-gather.13.cloned.1.call-done = f32[4096,128]{1,0:T(8,128)} async-done(((f32[1024,128]{1,0:T(8,128)}), f32[4096,128]{1,0:T(8,128)}) %all-gather.13.cloned.1.call-update) | async-done | bytes 2097168 | tf_op jit(solution)/shard_map/all_gather | solution.py:11
  458.1 1.8 reduce_sum.38
  459.8 1.6 fusion.25
  461.7 69.6 %all-reduce.17.cloned.1.call-done = f32[128,128]{0,1:T(8,128)} async-done(((f32[128,128]{0,1:T(8,128)}), f32[128,128]{0,1:T(8,128)}) %all-reduce.17.cloned.1.call-update) | async-done | bytes 65552 | tf_op jit(solution)/shard_map/psum | solution.py:38
  531.4 0.9 copy.11
  532.3 0.9 fusion.11
  533.2 11.7 %cholesky.96 = f32[128,128]{1,0:T(8,128)S(1)} custom-call(f32[128,128]{1,0:T(8,128)S(1)} %fusion.11), custom_call_target="Cholesky" | custom-call | tf_op jit(solution)/shard_map/jit(cholesky)/cholesky | solution.py:39
  545.6 0.7 fusion.18
  546.2 9.8 %custom-call.10 = f32[1,128,128]{1,2,0:T(8,128)S(1)} custom-call(f32[1,128,128]{2,1,0:T(8,128)S(1)} %get-tuple-element.15), custom_call_target="InvertDiagBlocksLowerTriangular" | custom-call | tf_op jit(solution)/shard_map/jit(_solve_triangular)/triangular_solve | solution.py:40
  556.7 5.4 fusion.26
  564.4 70.5 %all-reduce.19.cloned.1.call-done = f32[128,1024]{1,0:T(8,128)} async-done(((f32[128,1024]{1,0:T(8,128)}), f32[128,1024]{1,0:T(8,128)}) %all-reduce.19.cloned.1.call-update) | async-done | bytes 524304 | tf_op jit(solution)/shard_map/psum | solution.py:41
  634.9 5.5 convolution_subtract_fusion.1
  640.3 2.0 copy-done.3
  642.3 0.9 dynamic-slice_select_fusion
  643.3 21.9 %all-gather.15.cloned.1.call-done = f32[4096,128]{1,0:T(8,128)} async-done(((f32[1024,128]{1,0:T(8,128)}), f32[4096,128]{1,0:T(8,128)}) %all-gather.15.cloned.1.call-update) | async-done | bytes 2097168 | tf_op jit(solution)/shard_map/all_gather | solution.py:11
  665.1 1.8 reduce_sum.39
  666.9 1.6 fusion.27
  668.8 69.6 %all-reduce.21.cloned.1.call-done = f32[128,128]{0,1:T(8,128)} async-done(((f32[128,128]{0,1:T(8,128)}), f32[128,128]{0,1:T(8,128)}) %all-reduce.21.cloned.1.call-update) | async-done | bytes 65552 | tf_op jit(solution)/shard_map/psum | solution.py:38
  738.4 0.9 copy.13
  739.4 1.0 fusion.9
  740.4 11.7 %cholesky.107 = f32[128,128]{1,0:T(8,128)S(1)} custom-call(f32[128,128]{1,0:T(8,128)S(1)} %fusion.9), custom_call_target="Cholesky" | custom-call | tf_op jit(solution)/shard_map/jit(cholesky)/cholesky | solution.py:39
  752.8 0.7 select_bitcast_fusion
  753.4 9.8 %custom-call.11 = f32[1,128,128]{1,2,0:T(8,128)S(1)} custom-call(f32[1,128,128]{2,1,0:T(8,128)S(1)} %get-tuple-element.8), custom_call_target="InvertDiagBlocksLowerTriangular" | custom-call | tf_op jit(solution)/shard_map/jit(_solve_triangular)/triangular_solve | solution.py:40
  763.9 5.4 fusion.28
  769.3 0.8 copy.14
  770.2 72.0 %all-reduce.23.cloned.1.call-done = f32[128,1024]{1,0:T(8,128)} async-done(((f32[128,1024]{1,0:T(8,128)}), f32[128,1024]{1,0:T(8,128)}) %all-reduce.23.cloned.1.call-update) | async-done | bytes 524304 | tf_op jit(solution)/shard_map/psum | solution.py:41
  842.2 2.7 pad_maximum_fusion
  844.8 6.1 convolution_subtract_fusion
  (49 shorter events, 6.0 us)
Async XLA Ops:
  7.2 36.8 %all-gather.9.cloned.1.call-start = ((), (), s32[]{:S(2)}) async-start(), calls=%async_computation.8 | async-start | bytes 2621440 | tf_op jit(solution)/shard_map/all_gather | solution.py:11
  11.9 2.2 copy-start.5
  15.6 2.0 copy-start.2
  18.5 98.7 %all-reduce.9.cloned.1.call-start = ((), (), s32[]{:S(2)}) async-start(), calls=%async_computation | async-start | bytes 131072 | tf_op jit(solution)/shard_map/psum | solution.py:38
  47.4 173.5 %all-reduce.11.cloned.1.call-start = ((), (), s32[]{:S(2)}) async-start(), calls=%async_computation.1 | async-start | bytes 1048576 | tf_op jit(solution)/shard_map/psum | solution.py:41
  148.0 103.2 %all-gather.11.cloned.1.call-start = ((), (), s32[]{:S(2)}) async-start(), calls=%async_computation.9 | async-start | bytes 2621440 | tf_op jit(solution)/shard_map/all_gather | solution.py:11
  226.4 2.0 copy-start.1
  229.3 95.0 %all-reduce.13.cloned.1.call-start = ((), (), s32[]{:S(2)}) async-start(), calls=%async_computation.2 | async-start | bytes 131072 | tf_op jit(solution)/shard_map/psum | solution.py:38
  254.6 173.2 %all-reduce.15.cloned.1.call-start = ((), (), s32[]{:S(2)}) async-start(), calls=%async_computation.3 | async-start | bytes 1048576 | tf_op jit(solution)/shard_map/psum | solution.py:41
  355.0 103.1 %all-gather.13.cloned.1.call-start = ((), (), s32[]{:S(2)}) async-start(), calls=%async_computation.10 | async-start | bytes 2621440 | tf_op jit(solution)/shard_map/all_gather | solution.py:11
  433.3 2.0 copy-start
  436.2 95.2 %all-reduce.17.cloned.1.call-start = ((), (), s32[]{:S(2)}) async-start(), calls=%async_computation.4 | async-start | bytes 131072 | tf_op jit(solution)/shard_map/psum | solution.py:38
  461.5 173.4 %all-reduce.19.cloned.1.call-start = ((), (), s32[]{:S(2)}) async-start(), calls=%async_computation.5 | async-start | bytes 1048576 | tf_op jit(solution)/shard_map/psum | solution.py:41
  562.1 103.1 %all-gather.15.cloned.1.call-start = ((), (), s32[]{:S(2)}) async-start(), calls=%async_computation.11 | async-start | bytes 2621440 | tf_op jit(solution)/shard_map/all_gather | solution.py:11
  640.3 2.0 copy-start.3
  643.2 95.2 %all-reduce.21.cloned.1.call-start = ((), (), s32[]{:S(2)}) async-start(), calls=%async_computation.6 | async-start | bytes 131072 | tf_op jit(solution)/shard_map/psum | solution.py:38
  668.6 173.6 %all-reduce.23.cloned.1.call-start = ((), (), s32[]{:S(2)}) async-start(), calls=%async_computation.7 | async-start | bytes 1048576 | tf_op jit(solution)/shard_map/psum | solution.py:41
  739.4 102.8 %copy-start.6 = (f32[128,1024]{1,0:T(8,128)S(1)}, f32[128,1024]{1,0:T(8,128)}, u32[]{:S(2)}) copy-start(f32[128,1024]{1,0:T(8,128)} %all-reduce.11.cloned.1.call-done) | copy-start | bytes 1572868
  739.4 102.8 %copy-start.7 = (f32[128,1024]{1,0:T(8,128)S(1)}, f32[128,1024]{1,0:T(8,128)}, u32[]{:S(2)}) copy-start(f32[128,1024]{1,0:T(8,128)} %all-reduce.15.cloned.1.call-done) | copy-start | bytes 1572868
  739.4 102.8 %copy-start.8 = (f32[128,1024]{1,0:T(8,128)S(1)}, f32[128,1024]{1,0:T(8,128)}, u32[]{:S(2)}) copy-start(f32[128,1024]{1,0:T(8,128)} %all-reduce.19.cloned.1.call-done) | copy-start | bytes 1572868
  842.1 2.7 copy-start.4
Sparse Core Ops, SparseCore 0:
  18.7 25.2 all-gather.8
  48.0 69.2 all-reduce.8
  148.1 72.7 all-reduce.10
  229.4 21.7 all-gather.10
  255.0 69.2 all-reduce.12
  355.1 72.5 all-reduce.14
  436.3 21.7 all-gather.12
  462.1 69.2 all-reduce.16
  562.2 72.6 all-reduce.18
  643.4 21.7 all-gather.14
  669.1 69.2 all-reduce.20
  769.4 72.6 all-reduce.22
